TPU v7x, 32 devices: a whole 2x2x4 slice. The times are simulated.
32 devices in a mesh: exp: 4 (over x, core), fsdp: 8 (over z, y).
Axes of the slice: x: 2, y: 2, z: 4, core: 2. Of those that a mesh axis runs over, the one named last changes fastest.
Arguments:
- tokens: bfloat16 [8192, 1536], P(('exp', 'fsdp')), may hold values from -6 to 6
- cotangent: bfloat16 [8192, 1536], P(('exp', 'fsdp')), may hold values from -6 to 6
- prefix: int32 [32], P(('exp', 'fsdp')), may hold values from 25 to 128
- routes: int32 [8192, 8], P(('exp', 'fsdp')), may hold values from 0 to 19, all different within a row; in each aligned block of 256 rows (0 to 255, 256 to 511, ...) at most 128 rows name the same one
- attention_gain: bfloat16 [1536], P('fsdp'), may hold values from 0.5 to 1.5
- expert_gain: bfloat16 [1536], P('fsdp'), may hold values from 0.5 to 1.5
- query_weight: bfloat16 [1536, 1536], P('fsdp'), may hold values from -0.21875 to 0.21875
- key_weight: bfloat16 [1536, 512], P('fsdp'), may hold values from -0.21875 to 0.21875
- value_weight: bfloat16 [1536, 512], P('fsdp'), may hold values from -0.15625 to 0.15625
- output_weight: bfloat16 [1536, 1536], P('fsdp'), may hold values from -1.796875 to 1.796875
- router_weight: bfloat16 [1536, 20], P('fsdp'), may hold values from -0.078125 to 0.078125
- gate_weight: bfloat16 [20, 1536, 512], P('exp', 'fsdp'), may hold values from -0.15625 to 0.15625
- up_weight: bfloat16 [20, 1536, 512], P('exp', 'fsdp'), may hold values from -0.15625 to 0.15625
- down_weight: bfloat16 [20, 512, 1536], P('exp', 'fsdp'), may hold values from -4.1875 to 4.1875
Outputs:
- block_out: bfloat16 [8192, 1536], P(('exp', 'fsdp'))
- input_grad: float32 [8192, 1536], P(('exp', 'fsdp'))
- attention_gain_grad: float32 [1536], P('fsdp')
- expert_gain_grad: float32 [1536], P('fsdp')
- query_weight_grad: float32 [1536, 1536], P('fsdp')
- key_weight_grad: float32 [1536, 512], P('fsdp')
- value_weight_grad: float32 [1536, 512], P('fsdp')
- output_weight_grad: float32 [1536, 1536], P('fsdp')
- router_weight_grad: float32 [1536, 20], P('fsdp')
- gate_weight_grad: float32 [20, 1536, 512], P('exp', 'fsdp')
- up_weight_grad: float32 [20, 1536, 512], P('exp', 'fsdp')
- down_weight_grad: float32 [20, 512, 1536], P('exp', 'fsdp')
Inputs may be any that keep to these rules, and one draw needn't show every extreme that they name: `routes`: each row names 8 different experts. In the rows of one device no expert is named more than 128 times, a bound that some block reaches.
All inputs are finite; a program needn't handle non-finite values.
Results may differ from a plain program's by a relative error of at most 0.017.
Values may be sent and summed in bfloat16 or wider, within the bound.
No kernel may reach another device: no remote copies, remote signals or barrier semaphores. Data moves between devices by JAX's collectives and lax.ppermute only.
A program may use at most 192 MiB of HBM per device.

v0:
```python
import jax
import jax.numpy as jnp
from jax import lax
from jax.sharding import PartitionSpec as P

D = 1536
HEADS = 24
KV_HEADS = 8
HEAD = 64
TOP = 8
SEQ = 256
EXP_DEV = 5
CAP = 128


ATTENTION_SCALE = 0.015625
RESIDUAL_SCALE = 0.22
NORM_EPS = 1e-06
ROPE_BASE = 10000.0
MASKED = -1e30


def rotary(length):
    half_width = HEAD // 2
    frequency = ROPE_BASE ** (-(jnp.arange(half_width).astype(jnp.float32) * (2.0 / HEAD)))
    angles = jnp.arange(length).astype(jnp.float32)[:, None] * frequency[None, :]
    return (jnp.cos(angles)[:, None, :], jnp.sin(angles)[:, None, :])


def rotate(values, cosine, sine_table):
    half_width = values.shape[-1] // 2
    first_half = values[..., :half_width]
    second_half = values[..., half_width:]
    return jnp.concatenate(
        [
            first_half * cosine - second_half * sine_table,
            second_half * cosine + first_half * sine_table,
        ],
        axis=-1,
    )


def unrotate(values, cosine, sine_table):
    half_width = values.shape[-1] // 2
    first_half = values[..., :half_width]
    second_half = values[..., half_width:]
    return jnp.concatenate(
        [
            first_half * cosine + second_half * sine_table,
            second_half * cosine - first_half * sine_table,
        ],
        axis=-1,
    )


def on_device(
    tokens,
    cotangent,
    prefix,
    routes,
    attention_gain,
    expert_gain,
    query_weight,
    key_weight,
    value_weight,
    output_weight,
    router_weight,
    gate_weight,
    up_weight,
    down_weight,
):
    owners = lax.axis_size("exp")
    experts = EXP_DEV * owners
    length = tokens.shape[0]
    seq_count = length // SEQ
    group_size = HEADS // KV_HEADS
    group_width = group_size * HEAD
    dense_full = (
        lax.all_gather(query_weight, "fsdp", axis=0, tiled=True),
        lax.all_gather(key_weight, "fsdp", axis=0, tiled=True),
        lax.all_gather(value_weight, "fsdp", axis=0, tiled=True),
        lax.all_gather(output_weight, "fsdp", axis=0, tiled=True),
        lax.all_gather(router_weight, "fsdp", axis=0, tiled=True),
        lax.all_gather(attention_gain, "fsdp", axis=0, tiled=True),
        lax.all_gather(expert_gain, "fsdp", axis=0, tiled=True),
    )
    expert_full = (
        lax.all_gather(gate_weight, "fsdp", axis=1, tiled=True),
        lax.all_gather(up_weight, "fsdp", axis=1, tiled=True),
        lax.all_gather(down_weight, "fsdp", axis=1, tiled=True),
    )
    full_query, full_key, full_value, full_output, full_router, gain_one, gain_two = dense_full
    gate_full, up_full, down_full = expert_full
    inputs = tokens.astype(jnp.float32)
    scale_one = lax.rsqrt(jnp.mean(inputs * inputs, axis=-1, keepdims=True) + NORM_EPS)
    normed_one = (inputs * scale_one * gain_one.astype(jnp.float32)).astype(jnp.bfloat16)
    queries = jnp.dot(normed_one, full_query, preferred_element_type=jnp.float32)
    keys_raw = jnp.dot(normed_one, full_key, preferred_element_type=jnp.float32)
    values = jnp.dot(normed_one, full_value, preferred_element_type=jnp.float32).astype(
        jnp.bfloat16
    )
    cosine, sine_table = rotary(SEQ)
    queries_rot = (
        rotate(queries.reshape(seq_count, SEQ, HEADS, HEAD), cosine, sine_table)
        .astype(jnp.bfloat16)
        .reshape(length, HEADS * HEAD)
    )
    keys_rot = (
        rotate(keys_raw.reshape(seq_count, SEQ, KV_HEADS, HEAD), cosine, sine_table)
        .astype(jnp.bfloat16)
        .reshape(length, KV_HEADS * HEAD)
    )
    positions = jnp.arange(SEQ, dtype=jnp.int32)
    causal = positions[None, :] <= positions[:, None]
    visible = causal[None] | (positions[None, None, :] < prefix[:, None, None])
    visible_heads = visible[:, None]
    mixed_parts = []
    lse_parts = []
    for head_group in range(KV_HEADS):
        query_block = queries_rot[
            :, head_group * group_width : (head_group + 1) * group_width
        ].reshape(seq_count, SEQ, group_size, HEAD)
        key_block = keys_rot[:, head_group * HEAD : (head_group + 1) * HEAD].reshape(
            seq_count, SEQ, HEAD
        )
        value_block = values[:, head_group * HEAD : (head_group + 1) * HEAD].reshape(
            seq_count, SEQ, HEAD
        )
        scores = ATTENTION_SCALE * jnp.einsum(
            "bqgd,bpd->bgqp", query_block, key_block, preferred_element_type=jnp.float32
        )
        scores = jnp.where(visible_heads, scores, MASKED)
        highest = jnp.max(scores, axis=-1, keepdims=True)
        raised = jnp.exp(scores - highest)
        totals = jnp.sum(raised, axis=-1, keepdims=True)
        shares = (raised / totals).astype(jnp.bfloat16)
        lse_parts.append(highest + jnp.log(totals))
        mixed_parts.append(
            jnp.einsum(
                "bgqp,bpd->bqgd", shares, value_block, preferred_element_type=jnp.float32
            ).reshape(length, group_width)
        )
    mixed_heads = jnp.concatenate(mixed_parts, axis=1).astype(jnp.bfloat16)
    projected = jnp.dot(mixed_heads, full_output, preferred_element_type=jnp.float32)
    residual = inputs + RESIDUAL_SCALE * projected
    gain_two_float = gain_two.astype(jnp.float32)
    scale_two = lax.rsqrt(jnp.mean(residual * residual, axis=-1, keepdims=True) + NORM_EPS)
    normed_two = (residual * scale_two * gain_two_float).astype(jnp.bfloat16)
    flat_routes = routes.reshape(-1)
    expert_ids = jnp.arange(experts, dtype=jnp.int32)
    onehot = (flat_routes[:, None] == expert_ids[None, :]).astype(jnp.int32)
    slot_index = jnp.sum((jnp.cumsum(onehot, axis=0) - onehot) * onehot, axis=1)
    positions_flat = flat_routes * CAP + slot_index
    route_count = length * TOP
    sources = (
        jnp.full((experts * CAP,), route_count, jnp.int32)
        .at[positions_flat]
        .set(jnp.arange(route_count, dtype=jnp.int32))
    )
    padded = jnp.concatenate([normed_two, jnp.zeros((1, D), jnp.bfloat16)], axis=0)
    outgoing = padded[sources // TOP].reshape(owners, EXP_DEV * CAP, D)
    arrived = lax.all_to_all(outgoing, "exp", split_axis=0, concat_axis=0, tiled=True).reshape(
        owners, EXP_DEV, CAP, D
    )
    gate_value = jnp.einsum(
        "secd,edf->secf", arrived, gate_full, preferred_element_type=jnp.float32
    )
    up_value = jnp.einsum("secd,edf->secf", arrived, up_full, preferred_element_type=jnp.float32)
    gate_sigmoid = jax.nn.sigmoid(gate_value)
    activated = gate_value * gate_sigmoid
    hidden = (activated * up_value).astype(jnp.bfloat16)
    expert_out = jnp.einsum(
        "secf,efd->secd", hidden, down_full, preferred_element_type=jnp.float32
    ).astype(jnp.bfloat16)
    returned = lax.all_to_all(
        expert_out.reshape(owners, EXP_DEV * CAP, D), "exp", split_axis=0, concat_axis=0, tiled=True
    ).reshape(experts * CAP, D)
    picked = returned[positions_flat].reshape(length, TOP, D)
    logits = jnp.dot(normed_two, full_router, preferred_element_type=jnp.float32)
    route_onehot = (routes[:, :, None] == expert_ids[None, None, :]).astype(jnp.float32)
    chosen = jnp.sum(route_onehot * logits[:, None, :], axis=-1)
    gate_shares = jax.nn.softmax(chosen, axis=-1)
    mixture = jnp.sum(gate_shares[:, :, None] * picked.astype(jnp.float32), axis=1)
    block_out = (residual + RESIDUAL_SCALE * mixture).astype(jnp.bfloat16)
    dense_back = (
        lax.all_gather(query_weight, "fsdp", axis=0, tiled=True),
        lax.all_gather(key_weight, "fsdp", axis=0, tiled=True),
        lax.all_gather(value_weight, "fsdp", axis=0, tiled=True),
        lax.all_gather(output_weight, "fsdp", axis=0, tiled=True),
        lax.all_gather(router_weight, "fsdp", axis=0, tiled=True),
        lax.all_gather(attention_gain, "fsdp", axis=0, tiled=True),
        lax.all_gather(expert_gain, "fsdp", axis=0, tiled=True),
    )
    expert_back = (
        lax.all_gather(gate_weight, "fsdp", axis=1, tiled=True),
        lax.all_gather(up_weight, "fsdp", axis=1, tiled=True),
        lax.all_gather(down_weight, "fsdp", axis=1, tiled=True),
    )
    back_query, back_key, back_value, back_output, back_router, back_gain_one, back_gain_two = (
        dense_back
    )
    back_gate, back_up, back_down = expert_back
    upstream = cotangent.astype(jnp.float32)
    mix_grad = RESIDUAL_SCALE * upstream
    gate_grad = jnp.sum(mix_grad[:, None, :] * picked.astype(jnp.float32), axis=-1)
    choice_grad = gate_shares * (
        gate_grad - jnp.sum(gate_shares * gate_grad, axis=-1, keepdims=True)
    )
    logit_grad = jnp.sum(route_onehot * choice_grad[:, :, None], axis=1).astype(jnp.bfloat16)
    route_grads = (
        (gate_shares[:, :, None] * mix_grad[:, None, :])
        .astype(jnp.bfloat16)
        .reshape(route_count, D)
    )
    padded_grads = jnp.concatenate([route_grads, jnp.zeros((1, D), jnp.bfloat16)], axis=0)
    outgoing_grads = padded_grads[sources].reshape(owners, EXP_DEV * CAP, D)
    arrived_grads = lax.all_to_all(
        outgoing_grads, "exp", split_axis=0, concat_axis=0, tiled=True
    ).reshape(owners, EXP_DEV, CAP, D)
    hidden_grad = jnp.einsum(
        "secd,efd->secf", arrived_grads, back_down, preferred_element_type=jnp.float32
    )
    down_w_grad = jnp.einsum(
        "secf,secd->efd", hidden, arrived_grads, preferred_element_type=jnp.float32
    )
    gate_pre_grad = (
        hidden_grad * up_value * gate_sigmoid * (1.0 + gate_value * (1.0 - gate_sigmoid))
    ).astype(jnp.bfloat16)
    up_pre_grad = (hidden_grad * activated).astype(jnp.bfloat16)
    gate_w_grad = jnp.einsum(
        "secd,secf->edf", arrived, gate_pre_grad, preferred_element_type=jnp.float32
    )
    up_w_grad = jnp.einsum(
        "secd,secf->edf", arrived, up_pre_grad, preferred_element_type=jnp.float32
    )
    row_grads = (
        jnp.einsum("secf,edf->secd", gate_pre_grad, back_gate, preferred_element_type=jnp.float32)
        + jnp.einsum("secf,edf->secd", up_pre_grad, back_up, preferred_element_type=jnp.float32)
    ).astype(jnp.bfloat16)
    back_rows = lax.all_to_all(
        row_grads.reshape(owners, EXP_DEV * CAP, D), "exp", split_axis=0, concat_axis=0, tiled=True
    ).reshape(experts * CAP, D)
    normed_two_grad = jnp.sum(
        back_rows[positions_flat].reshape(length, TOP, D).astype(jnp.float32), axis=1
    )
    normed_two_grad = normed_two_grad + jnp.einsum(
        "te,de->td", logit_grad, back_router, preferred_element_type=jnp.float32
    )
    router_w_grad = jnp.einsum(
        "td,te->de", normed_two, logit_grad, preferred_element_type=jnp.float32
    )
    inner_two = normed_two_grad * back_gain_two.astype(jnp.float32)
    expert_gain_grad = jnp.sum(normed_two_grad * residual * scale_two, axis=0)
    cube_two = scale_two * scale_two * scale_two
    residual_grad = (
        upstream
        + scale_two * inner_two
        - residual * cube_two * jnp.mean(inner_two * residual, axis=-1, keepdims=True)
    )
    proj_grad = (RESIDUAL_SCALE * residual_grad).astype(jnp.bfloat16)
    output_w_grad = jnp.einsum(
        "tf,td->fd", mixed_heads, proj_grad, preferred_element_type=jnp.float32
    )
    mixed_grad = jnp.einsum(
        "td,fd->tf", proj_grad, back_output, preferred_element_type=jnp.float32
    ).astype(jnp.bfloat16)
    query_parts = []
    key_parts = []
    value_parts = []
    for head_group in range(KV_HEADS):
        query_block = queries_rot[
            :, head_group * group_width : (head_group + 1) * group_width
        ].reshape(seq_count, SEQ, group_size, HEAD)
        key_block = keys_rot[:, head_group * HEAD : (head_group + 1) * HEAD].reshape(
            seq_count, SEQ, HEAD
        )
        value_block = values[:, head_group * HEAD : (head_group + 1) * HEAD].reshape(
            seq_count, SEQ, HEAD
        )
        grad_block = mixed_grad[
            :, head_group * group_width : (head_group + 1) * group_width
        ].reshape(seq_count, SEQ, group_size, HEAD)
        scores = ATTENTION_SCALE * jnp.einsum(
            "bqgd,bpd->bgqp", query_block, key_block, preferred_element_type=jnp.float32
        )
        scores = jnp.where(visible_heads, scores, MASKED)
        shares_float = jnp.exp(scores - lse_parts[head_group])
        shares = shares_float.astype(jnp.bfloat16)
        share_grad = jnp.einsum(
            "bqgd,bpd->bgqp", grad_block, value_block, preferred_element_type=jnp.float32
        )
        row_delta = jnp.sum(shares_float * share_grad, axis=-1, keepdims=True)
        score_grad = (shares_float * (share_grad - row_delta)).astype(jnp.bfloat16)
        query_parts.append(
            ATTENTION_SCALE
            * jnp.einsum(
                "bgqp,bpd->bqgd", score_grad, key_block, preferred_element_type=jnp.float32
            ).reshape(length, group_width)
        )
        key_parts.append(
            ATTENTION_SCALE
            * jnp.einsum(
                "bgqp,bqgd->bpd", score_grad, query_block, preferred_element_type=jnp.float32
            ).reshape(length, HEAD)
        )
        value_parts.append(
            jnp.einsum(
                "bgqp,bqgd->bpd", shares, grad_block, preferred_element_type=jnp.float32
            ).reshape(length, HEAD)
        )
    query_grad = (
        unrotate(
            jnp.concatenate(query_parts, axis=1).reshape(seq_count, SEQ, HEADS, HEAD),
            cosine,
            sine_table,
        )
        .reshape(length, HEADS * HEAD)
        .astype(jnp.bfloat16)
    )
    key_grad = (
        unrotate(
            jnp.concatenate(key_parts, axis=1).reshape(seq_count, SEQ, KV_HEADS, HEAD),
            cosine,
            sine_table,
        )
        .reshape(length, KV_HEADS * HEAD)
        .astype(jnp.bfloat16)
    )
    value_grad = jnp.concatenate(value_parts, axis=1).astype(jnp.bfloat16)
    query_w_grad = jnp.einsum(
        "td,tf->df", normed_one, query_grad, preferred_element_type=jnp.float32
    )
    key_w_grad = jnp.einsum("td,tf->df", normed_one, key_grad, preferred_element_type=jnp.float32)
    value_w_grad = jnp.einsum(
        "td,tf->df", normed_one, value_grad, preferred_element_type=jnp.float32
    )
    normed_one_grad = (
        jnp.einsum("tf,df->td", query_grad, back_query, preferred_element_type=jnp.float32)
        + jnp.einsum("tf,df->td", key_grad, back_key, preferred_element_type=jnp.float32)
        + jnp.einsum("tf,df->td", value_grad, back_value, preferred_element_type=jnp.float32)
    )
    inner_one = normed_one_grad * back_gain_one.astype(jnp.float32)
    attention_gain_grad = jnp.sum(normed_one_grad * inputs * scale_one, axis=0)
    cube_one = scale_one * scale_one * scale_one
    input_grad = (
        residual_grad
        + scale_one * inner_one
        - inputs * cube_one * jnp.mean(inner_one * inputs, axis=-1, keepdims=True)
    )
    gate_sum, up_sum, down_sum = (
        lax.psum_scatter(gate_w_grad, "fsdp", scatter_dimension=1, tiled=True),
        lax.psum_scatter(up_w_grad, "fsdp", scatter_dimension=1, tiled=True),
        lax.psum_scatter(down_w_grad, "fsdp", scatter_dimension=1, tiled=True),
    )
    query_part, key_part, value_part, output_part, router_part, gain_one_part, gain_two_part = (
        lax.psum_scatter(query_w_grad, "fsdp", scatter_dimension=0, tiled=True),
        lax.psum_scatter(key_w_grad, "fsdp", scatter_dimension=0, tiled=True),
        lax.psum_scatter(value_w_grad, "fsdp", scatter_dimension=0, tiled=True),
        lax.psum_scatter(output_w_grad, "fsdp", scatter_dimension=0, tiled=True),
        lax.psum_scatter(router_w_grad, "fsdp", scatter_dimension=0, tiled=True),
        lax.psum_scatter(attention_gain_grad, "fsdp", scatter_dimension=0, tiled=True),
        lax.psum_scatter(expert_gain_grad, "fsdp", scatter_dimension=0, tiled=True),
    )
    query_sum, key_sum, value_sum, output_sum, router_sum, gain_one_sum, gain_two_sum = lax.psum(
        (query_part, key_part, value_part, output_part, router_part, gain_one_part, gain_two_part),
        "exp",
    )
    return (
        block_out,
        input_grad,
        gain_one_sum,
        gain_two_sum,
        query_sum,
        key_sum,
        value_sum,
        output_sum,
        router_sum,
        gate_sum,
        up_sum,
        down_sum,
    )


def solution(mesh):
    in_specs = (
        P(("exp", "fsdp"), None),
        P(("exp", "fsdp"), None),
        P(("exp", "fsdp")),
        P(("exp", "fsdp"), None),
        P("fsdp"),
        P("fsdp"),
        P("fsdp", None),
        P("fsdp", None),
        P("fsdp", None),
        P("fsdp", None),
        P("fsdp", None),
        P("exp", "fsdp", None),
        P("exp", "fsdp", None),
        P("exp", "fsdp", None),
    )
    out_specs = (
        P(("exp", "fsdp"), None),
        P(("exp", "fsdp"), None),
        P("fsdp"),
        P("fsdp"),
        P("fsdp", None),
        P("fsdp", None),
        P("fsdp", None),
        P("fsdp", None),
        P("fsdp", None),
        P("exp", "fsdp", None),
        P("exp", "fsdp", None),
        P("exp", "fsdp", None),
    )
    return jax.shard_map(
        on_device, mesh=mesh, in_specs=in_specs, out_specs=out_specs, check_vma=False
    )
```

profile of v0, /device:TPU:0, one launch (start us, length us, event | category | flops | bytes accessed | tf_op | source)
XLA Modules:
  0.0 2272.6 jit_solution(2168573660228298233)
XLA Ops:
  15.7 23.4 %all-reduce.9 = (bf16[1536]{0:T(1024)(128)(2,1)S(1)}, bf16[1536]{0:T(1024)(128)(2,1)S(1)}) all-reduce(bf16[1536]{0:T(1024)(128)(2,1)S(1)} %dynamic-update-slice, bf16[1536]{0:T(1024)(128)(2,1)S(1)} %dynamic-update-slice.1), channel_id=1, replica_groups=mesh['exp'=4,'fsdp'=8] {'fsdp'}, use_global_device_ids=true, to_apply=%add.2 | all-reduce | flops 3072 | bytes 12288
  59.6 42.4 %all-gather.9.cloned.1.call-done = bf16[1536,512]{1,0:T(8,128)(2,1)} async-done(((bf16[192,512]{1,0:T(8,128)(2,1)}), bf16[1536,512]{1,0:T(8,128)(2,1)}) %all-gather.9.cloned.1.call-update) | async-done | bytes 1572880 | tf_op jit(solution)/shard_map/all_gather | solution.py:81
  104.0 77.9 %all-gather.13.cloned.1.call-done = bf16[1536,1536]{1,0:T(8,128)(2,1)} async-done(((bf16[192,1536]{1,0:T(8,128)(2,1)}), bf16[1536,1536]{1,0:T(8,128)(2,1)}) %all-gather.13.cloned.1.call-update) | async-done | bytes 4718608 | tf_op jit(solution)/shard_map/all_gather | solution.py:79
  195.8 65.9 %all-gather.15.cloned.1.call-done = bf16[1536,1536]{1,0:T(8,128)(2,1)} async-done(((bf16[192,1536]{1,0:T(8,128)(2,1)}), bf16[1536,1536]{1,0:T(8,128)(2,1)}) %all-gather.15.cloned.1.call-update) | async-done | bytes 4718608 | tf_op jit(solution)/shard_map/all_gather | solution.py:82
  282.0 42.3 %all-gather = bf16[8,192,20]{1,2,0:T(8,128)(2,1)S(1)} all-gather(bf16[1,192,20]{1,2,0:T(8,128)(2,1)S(1)} %bitcast.728), channel_id=1, replica_groups=mesh['exp'=4,'fsdp'=8] {'fsdp'}, dimensions={0}, use_global_device_ids=true | all-gather | bytes 69120 | tf_op jit(solution)/shard_map/all_gather | solution.py:83
  330.3 20.0 gather_fusion.2
  350.3 19.3 all-to-all-done
  393.0 106.3 %all-gather.17.cloned.1.call-done = bf16[5,1536,512]{2,1,0:T(8,128)(2,1)} async-done(((bf16[5,192,512]{2,1,0:T(8,128)(2,1)}), bf16[5,1536,512]{2,1,0:T(8,128)(2,1)}) %all-gather.17.cloned.1.call-update) | async-done | bytes 7864336 | tf_op jit(solution)/shard_map/all_gather | solution.py:88
  511.2 106.3 %all-gather.21.cloned.1.call-done = bf16[5,512,1536]{2,1,0:T(8,128)(2,1)} async-done(((bf16[5,64,1536]{2,1,0:T(8,128)(2,1)}), bf16[5,512,1536]{2,1,0:T(8,128)(2,1)}) %all-gather.21.cloned.1.call-update) | async-done | bytes 7864336 | tf_op jit(solution)/shard_map/all_gather | solution.py:90
  689.5 53.7 %all-to-all-done.1 = bf16[4,640,1536]{2,1,0:T(8,128)(2,1)} async-done(((bf16[4,640,1536]{2,1,0:T(8,128)(2,1)}), bf16[4,640,1536]{2,1,0:T(8,128)(2,1)}, u32[]{:S(2)}, u32[]{:S(2)}) %all-to-all-start.1) | async-done | bytes 7864352 | tf_op jit(solution)/shard_map/all_to_all | solution.py:175
  749.2 17.5 gather_fusion.1
  776.4 60.1 %all-to-all-done.3 = bf16[4,640,1536]{2,1,0:T(8,128)(2,1)} async-done(((bf16[4,640,1536]{2,1,0:T(8,128)(2,1)}), bf16[4,640,1536]{2,1,0:T(8,128)(2,1)}, u32[]{:S(2)}, u32[]{:S(2)}) %all-to-all-start.3) | async-done | bytes 7864352 | tf_op jit(solution)/shard_map/all_to_all | solution.py:240
  836.4 17.7 gather_fusion.3
  918.6 34.7 %reduce-scatter.15.cloned.1.call-done = f32[192,512]{1,0:T(8,128)} async-done(((f32[1536,512]{1,0:T(8,128)}), f32[192,512]{1,0:T(8,128)}) %reduce-scatter.15.cloned.1.call-update) | async-done | bytes 393232 | tf_op jit(solution)/shard_map/reduce_scatter | solution.py:358
  953.2 77.1 %reduce-scatter.13.cloned.1.call-done = f32[192,512]{1,0:T(8,128)} async-done(((f32[1536,512]{1,0:T(8,128)}), f32[192,512]{1,0:T(8,128)}) %reduce-scatter.13.cloned.1.call-update) | async-done | bytes 393232 | tf_op jit(solution)/shard_map/reduce_scatter | solution.py:357
  1030.3 164.7 %reduce-scatter.17.cloned.1.call-done = f32[192,1536]{1,0:T(8,128)} async-done(((f32[1536,1536]{1,0:T(8,128)}), f32[192,1536]{1,0:T(8,128)}) %reduce-scatter.17.cloned.1.call-update) | async-done | bytes 1179664 | tf_op jit(solution)/shard_map/reduce_scatter | solution.py:359
  1195.0 164.8 %reduce-scatter.11.cloned.1.call-done = f32[192,1536]{1,0:T(8,128)} async-done(((f32[1536,1536]{1,0:T(8,128)}), f32[192,1536]{1,0:T(8,128)}) %reduce-scatter.11.cloned.1.call-update) | async-done | bytes 1179664 | tf_op jit(solution)/shard_map/reduce_scatter | solution.py:356
  1374.1 13.8 convolution_bitcast_fusion.2
  1388.2 13.8 convolution_bitcast_fusion.1
  1410.6 35.2 %all-reduce.6 = (f32[1536]{0:T(1024)S(1)}, f32[1536]{0:T(1024)S(1)}) all-reduce(f32[1536]{0:T(1024)S(1)} %get-tuple-element.16, f32[1536]{0:T(1024)S(1)} %copy-done.117), channel_id=2, replica_groups=mesh['exp'=4,'fsdp'=8] {'fsdp'}, use_global_device_ids=true, to_apply=%region_41.42.clone | all-reduce | flops 3072 | bytes 24576
  1462.5 34.1 %all-reduce.12.cloned.1.call-done = (f32[192,1536]{1,0:T(8,128)}, f32[192,512]{1,0:T(8,128)}, f32[192,512]{1,0:T(8,128)}, f32[192,1536]{1,0:T(8,128)}) async-done(((f32[192,1536]{1,0:T(8,128)}, f32[192,512]{1,0:T(8,128)}, f32[192,512]{1,0:T(8,128)}, f32[192,1536]{1,0:T(8,128)}), (f32[192,1536]{1,0:T(8,128)}, f32[192,512]{1,0:T(8,128)}, f32[192,512]{1,0:T(8,128)}, ...) | async-done | bytes 3145744 | tf_op jit(solution)/shard_map/psum | solution.py:364
  1496.6 255.4 %reduce-scatter.23.cloned.1.call-done = f32[5,64,1536]{2,1,0:T(8,128)} async-done(((f32[5,512,1536]{2,1,0:T(8,128)}), f32[5,64,1536]{2,1,0:T(8,128)}) %reduce-scatter.23.cloned.1.call-update) | async-done | bytes 1966096 | tf_op jit(solution)/shard_map/reduce_scatter | solution.py:353
  1752.0 254.4 %reduce-scatter.19.cloned.1.call-done = f32[5,192,512]{2,1,0:T(8,128)} async-done(((f32[5,1536,512]{2,1,0:T(8,128)}), f32[5,192,512]{2,1,0:T(8,128)}) %reduce-scatter.19.cloned.1.call-update) | async-done | bytes 1966096 | tf_op jit(solution)/shard_map/reduce_scatter | solution.py:351
  2006.4 254.4 %reduce-scatter.21.cloned.1.call-done = f32[5,192,512]{2,1,0:T(8,128)} async-done(((f32[5,1536,512]{2,1,0:T(8,128)}), f32[5,192,512]{2,1,0:T(8,128)}) %reduce-scatter.21.cloned.1.call-update) | async-done | bytes 1966096 | tf_op jit(solution)/shard_map/reduce_scatter | solution.py:352
  (499 shorter events, 299.2 us)
Async XLA Ops:
  7.2 50.1 %all-gather.11.cloned.1.call-start = ((), (), s32[]{:S(2)}) async-start(), calls=%async_computation.13 | async-start | bytes 1769472 | tf_op jit(solution)/shard_map/all_gather | solution.py:80
  7.9 94.1 %all-gather.9.cloned.1.call-start = ((), (), s32[]{:S(2)}) async-start(), calls=%async_computation.12 | async-start | bytes 1769472 | tf_op jit(solution)/shard_map/all_gather | solution.py:81
  8.7 173.2 %all-gather.13.cloned.1.call-start = ((), (), s32[]{:S(2)}) async-start(), calls=%async_computation.14 | async-start | bytes 5308416 | tf_op jit(solution)/shard_map/all_gather | solution.py:79
  9.4 252.3 %all-gather.15.cloned.1.call-start = ((), (), s32[]{:S(2)}) async-start(), calls=%async_computation.15 | async-start | bytes 5308416 | tf_op jit(solution)/shard_map/all_gather | solution.py:82
  10.0 371.0 %all-gather.19.cloned.1.call-start = ((), (), s32[]{:S(2)}) async-start(), calls=%async_computation.17 | async-start | bytes 8847360 | tf_op jit(solution)/shard_map/all_gather | solution.py:89
  10.6 488.6 %all-gather.17.cloned.1.call-start = ((), (), s32[]{:S(2)}) async-start(), calls=%async_computation.16 | async-start | bytes 8847360 | tf_op jit(solution)/shard_map/all_gather | solution.py:88
  11.2 606.4 %all-gather.21.cloned.1.call-start = ((), (), s32[]{:S(2)}) async-start(), calls=%async_computation.18 | async-start | bytes 8847360 | tf_op jit(solution)/shard_map/all_gather | solution.py:90
  13.8 168.1 %copy-start.114 = (f32[256]{0:T(256)}, f32[256]{0:T(256)S(1)}, u32[]{:S(2)}) copy-start(f32[256]{0:T(256)S(1)} %get-tuple-element.63) | copy-start | bytes 3076
  39.1 142.8 %copy-start.96 = (f32[1536]{0:T(1024)}, f32[1536]{0:T(1024)S(1)}, u32[]{:S(2)}) copy-start(f32[1536]{0:T(1024)S(1)} %convert_element_type.256) | copy-start | bytes 18436
  39.1 227.1 %copy-start.99 = (f32[1536]{0:T(1024)}, f32[1536]{0:T(1024)S(1)}, u32[]{:S(2)}) copy-start(f32[1536]{0:T(1024)S(1)} %convert_element_type.271) | copy-start | bytes 18436
  276.3 93.2 %all-to-all-start = ((bf16[4,640,1536]{2,1,0:T(8,128)(2,1)}), bf16[4,640,1536]{2,1,0:T(8,128)(2,1)}, u32[]{:S(2)}, u32[]{:S(2)}) async-start(bf16[4,640,1536]{2,1,0:T(8,128)(2,1)} %bitcast.643), calls=%async_computation | async-start | bytes 15728640 | tf_op jit(solution)/shard_map/all_to_all | solution.py:162
  369.5 248.1 %all-to-all-start.2 = ((bf16[4,640,1536]{2,1,0:T(8,128)(2,1)}), bf16[4,640,1536]{2,1,0:T(8,128)(2,1)}, u32[]{:S(2)}, u32[]{:S(2)}) async-start(bf16[4,640,1536]{2,1,0:T(8,128)(2,1)} %bitcast.644), calls=%async_computation.2 | async-start | bytes 15728640 | tf_op jit(solution)/shard_map/all_to_all | solution.py:217
  649.7 93.4 %all-to-all-start.1 = ((bf16[4,640,1536]{2,1,0:T(8,128)(2,1)}), bf16[4,640,1536]{2,1,0:T(8,128)(2,1)}, u32[]{:S(2)}, u32[]{:S(2)}) async-start(bf16[4,640,1536]{2,1,0:T(8,128)(2,1)} %bitcast.645), calls=%async_computation.1 | async-start | bytes 15728640 | tf_op jit(solution)/shard_map/all_to_all | solution.py:175
  743.2 93.2 %all-to-all-start.3 = ((bf16[4,640,1536]{2,1,0:T(8,128)(2,1)}), bf16[4,640,1536]{2,1,0:T(8,128)(2,1)}, u32[]{:S(2)}, u32[]{:S(2)}) async-start(bf16[4,640,1536]{2,1,0:T(8,128)(2,1)} %bitcast.642), calls=%async_computation.3 | async-start | bytes 15728640 | tf_op jit(solution)/shard_map/all_to_all | solution.py:240
  748.9 204.3 %reduce-scatter.15.cloned.1.call-start = ((), (), s32[]{:S(2)}) async-start(), calls=%async_computation.21 | async-start | bytes 3538944 | tf_op jit(solution)/shard_map/reduce_scatter | solution.py:358
  881.5 148.9 %reduce-scatter.13.cloned.1.call-start = ((), (), s32[]{:S(2)}) async-start(), calls=%async_computation.20 | async-start | bytes 3538944 | tf_op jit(solution)/shard_map/reduce_scatter | solution.py:357
  899.0 296.0 %reduce-scatter.17.cloned.1.call-start = ((), (), s32[]{:S(2)}) async-start(), calls=%async_computation.22 | async-start | bytes 10616832 | tf_op jit(solution)/shard_map/reduce_scatter | solution.py:359
  905.7 454.2 %reduce-scatter.11.cloned.1.call-start = ((), (), s32[]{:S(2)}) async-start(), calls=%async_computation.19 | async-start | bytes 10616832 | tf_op jit(solution)/shard_map/reduce_scatter | solution.py:356
  916.1 532.9 %reduce-scatter.25.cloned.1.call-start = ((), (), s32[]{:S(2)}) async-start(), calls=%async_computation.26 | async-start | bytes 884736
  918.5 578.0 %all-reduce.12.cloned.1.call-start = ((), (), s32[]{:S(2)}) async-start(), calls=%async_computation.27 | async-start | bytes 6291456 | tf_op jit(solution)/shard_map/psum | solution.py:364
  1359.8 392.2 %reduce-scatter.23.cloned.1.call-start = ((), (), s32[]{:S(2)}) async-start(), calls=%async_computation.25 | async-start | bytes 17694720 | tf_op jit(solution)/shard_map/reduce_scatter | solution.py:353
  1374.1 632.4 %reduce-scatter.19.cloned.1.call-start = ((), (), s32[]{:S(2)}) async-start(), calls=%async_computation.23 | async-start | bytes 17694720 | tf_op jit(solution)/shard_map/reduce_scatter | solution.py:351
  1388.0 872.9 %reduce-scatter.21.cloned.1.call-start = ((), (), s32[]{:S(2)}) async-start(), calls=%async_computation.24 | async-start | bytes 17694720 | tf_op jit(solution)/shard_map/reduce_scatter | solution.py:352
  1496.6 766.8 %copy-start.95 = (f32[192,512]{1,0:T(8,128)S(1)}, f32[192,512]{1,0:T(8,128)}, u32[]{:S(2)}) copy-start(f32[192,512]{1,0:T(8,128)} %get-tuple-element.111) | copy-start | bytes 1179652
  (126 other events, 1851.4 us)
Sparse Core Ops, SparseCore 0:
  10.2 47.0 all-gather.10
  59.4 42.5 all-gather.8
  104.2 77.6 all-gather.12
  183.9 77.7 all-gather.14
  263.8 117.2 all-gather.18
  383.0 116.1 all-gather.16
  501.4 116.0 all-gather.20
  881.6 71.6 reduce-scatter.14
  956.8 73.4 reduce-scatter.12
  1033.8 161.1 reduce-scatter.16
  1198.6 161.1 reduce-scatter.10
  1363.5 62.3 reduce-scatter.24
  1428.5 68.0 all-reduce.11
  1500.6 251.3 reduce-scatter.22
  1756.0 250.3 reduce-scatter.18
  2010.5 250.3 reduce-scatter.20
where the time goes:
time: 2280 us; the launch traced here: 2270 us
  waiting for transfers between devices  1780 us (78%)
  matrix products  172 us (8%)
  local copies, waits for them, and re-layouts  125 us (5%)
  blocking collectives  114 us (5%)
  other arithmetic  35.3 us (2%)
  starting transfers between devices  24.3 us (1%)
    reduce_scatter x1, waiting for transfers between devices, on_device(): lax.psum_scatter(down_w_grad, 'fsdp', scatter_dimension=1, tiled=True)  255 us
    reduce_scatter x1, waiting for transfers between devices, on_device(): lax.psum_scatter(up_w_grad, 'fsdp', scatter_dimension=1, tiled=True)  254 us
    reduce_scatter x1, waiting for transfers between devices, on_device(): lax.psum_scatter(gate_w_grad, 'fsdp', scatter_dimension=1, tiled=True)  254 us
    reduce_scatter x1, waiting for transfers between devices, on_device(): lax.psum_scatter(query_w_grad, 'fsdp', scatter_dimension=0, tiled=True)  165 us
    reduce_scatter x1, waiting for transfers between devices, on_device(): lax.psum_scatter(output_w_grad, 'fsdp', scatter_dimension=0, tiled=True)  165 us
    all_gather x1, waiting for transfers between devices, on_device(): lax.all_gather(down_weight, 'fsdp', axis=1, tiled=True)  106 us
    all_gather x1, waiting for transfers between devices, on_device(): lax.all_gather(gate_weight, 'fsdp', axis=1, tiled=True)  106 us
    all_gather x1, waiting for transfers between devices, on_device(): lax.all_gather(query_weight, 'fsdp', axis=0, tiled=True)  77.9 us
  transfers between devices with their start and end apart: 20, of which 18 were waited for; matrix products, arithmetic and copies ran while one was open for 10% of the time, Pallas kernels for 0%

commit v1 on v0

v1 whole, which is shorter than its diff:
```python
import jax
import jax.numpy as jnp
from jax import lax
from jax.sharding import PartitionSpec as P

D = 1536
HEADS = 24
KV_HEADS = 8
HEAD = 64
TOP = 8
SEQ = 256
EXP_DEV = 5
CAP = 128
QKV = (HEADS + 2 * KV_HEADS) * HEAD
MISC = 128

ATTENTION_SCALE = 0.015625
RESIDUAL_SCALE = 0.22
NORM_EPS = 1e-06
ROPE_BASE = 10000.0
MASKED = -1e30

BF = jnp.bfloat16
F32 = jnp.float32


def rotary(length):
    half_width = HEAD // 2
    frequency = ROPE_BASE ** (-(jnp.arange(half_width).astype(jnp.float32) * (2.0 / HEAD)))
    angles = jnp.arange(length).astype(jnp.float32)[:, None] * frequency[None, :]
    return (jnp.cos(angles)[:, None, :], jnp.sin(angles)[:, None, :])


def rotate(values, cosine, sine_table):
    half_width = values.shape[-1] // 2
    first_half = values[..., :half_width]
    second_half = values[..., half_width:]
    return jnp.concatenate(
        [
            first_half * cosine - second_half * sine_table,
            second_half * cosine + first_half * sine_table,
        ],
        axis=-1,
    )


def unrotate(values, cosine, sine_table):
    half_width = values.shape[-1] // 2
    first_half = values[..., :half_width]
    second_half = values[..., half_width:]
    return jnp.concatenate(
        [
            first_half * cosine + second_half * sine_table,
            second_half * cosine - first_half * sine_table,
        ],
        axis=-1,
    )


def swap(values, bit):
    size = lax.axis_size("exp")
    return lax.ppermute(values, "exp", [(i, i ^ bit) for i in range(size)])


def gather_exp(values):
    far = swap(values, 2)
    near = swap(values, 1)
    both = swap(far, 1)
    return [values, near, far, both]


def scatter_exp(parts):
    near = swap(jnp.stack([parts[1].astype(BF), parts[3].astype(BF)]), 1)
    mine = parts[0] + near[0].astype(F32)
    other = (parts[2] + near[1].astype(F32)).astype(BF)
    return mine + swap(other, 2).astype(F32)


def ordered(blocks, me, axis):
    count = len(blocks)
    width = blocks[0].shape[axis]
    shape = list(blocks[0].shape)
    shape[axis] = width * count
    out = jnp.zeros(shape, blocks[0].dtype)
    for j, block in enumerate(blocks):
        out = lax.dynamic_update_slice_in_dim(out, block, (me ^ j) * width, axis)
    return out


def on_device(
    tokens,
    cotangent,
    prefix,
    routes,
    attention_gain,
    expert_gain,
    query_weight,
    key_weight,
    value_weight,
    output_weight,
    router_weight,
    gate_weight,
    up_weight,
    down_weight,
):
    owners = lax.axis_size("exp")
    shards = lax.axis_size("fsdp")
    me = lax.axis_index("exp")
    experts = EXP_DEV * owners
    length = tokens.shape[0]
    seq_count = length // SEQ
    group_size = HEADS // KV_HEADS
    group_width = group_size * HEAD
    piece = query_weight.shape[0] // owners

    def own_rows(weight):
        return lax.dynamic_slice_in_dim(weight, me * piece, piece, 0)

    misc = jnp.concatenate(
        [
            router_weight,
            attention_gain[:, None],
            expert_gain[:, None],
            jnp.zeros((router_weight.shape[0], MISC - experts - 2), BF),
        ],
        axis=1,
    )
    dense_piece = jnp.concatenate(
        [
            own_rows(w)
            for w in (query_weight, key_weight, value_weight, misc, output_weight)
        ],
        axis=1,
    )
    dense_quarter = lax.all_gather(dense_piece, "fsdp", axis=0, tiled=False)
    first_cols = QKV + MISC
    full_first = ordered(gather_exp(dense_quarter[:, :, :first_cols]), me, 1).reshape(D, first_cols)
    full_output = ordered(gather_exp(dense_quarter[:, :, first_cols:]), me, 1).reshape(D, D)
    full_qkv = full_first[:, :QKV]
    full_router = full_first[:, QKV : QKV + experts]
    gain_one = full_first[:, QKV + experts].astype(F32)
    gain_two = full_first[:, QKV + experts + 1].astype(F32)
    gate_full = lax.all_gather(gate_weight, "fsdp", axis=1, tiled=True)
    up_full = lax.all_gather(up_weight, "fsdp", axis=1, tiled=True)
    down_full = lax.all_gather(down_weight, "fsdp", axis=1, tiled=True)

    route_blocks = jnp.stack(gather_exp(routes))
    upstream_blocks = jnp.stack(gather_exp(cotangent))

    inputs = tokens.astype(F32)
    scale_one = lax.rsqrt(jnp.mean(inputs * inputs, axis=-1, keepdims=True) + NORM_EPS)
    normed_one = (inputs * scale_one * gain_one).astype(BF)
    projections = jnp.dot(normed_one, full_qkv, preferred_element_type=F32)
    queries = projections[:, : HEADS * HEAD]
    keys_raw = projections[:, HEADS * HEAD : (HEADS + KV_HEADS) * HEAD]
    values = projections[:, (HEADS + KV_HEADS) * HEAD :].astype(BF)
    cosine, sine_table = rotary(SEQ)
    queries_rot = (
        rotate(queries.reshape(seq_count, SEQ, HEADS, HEAD), cosine, sine_table)
        .astype(BF)
        .reshape(length, HEADS * HEAD)
    )
    keys_rot = (
        rotate(keys_raw.reshape(seq_count, SEQ, KV_HEADS, HEAD), cosine, sine_table)
        .astype(BF)
        .reshape(length, KV_HEADS * HEAD)
    )
    positions = jnp.arange(SEQ, dtype=jnp.int32)
    causal = positions[None, :] <= positions[:, None]
    visible = causal[None] | (positions[None, None, :] < prefix[:, None, None])
    visible_heads = visible[:, None]
    mixed_parts = []
    lse_parts = []
    for head_group in range(KV_HEADS):
        query_block = queries_rot[
            :, head_group * group_width : (head_group + 1) * group_width
        ].reshape(seq_count, SEQ, group_size, HEAD)
        key_block = keys_rot[:, head_group * HEAD : (head_group + 1) * HEAD].reshape(
            seq_count, SEQ, HEAD
        )
        value_block = values[:, head_group * HEAD : (head_group + 1) * HEAD].reshape(
            seq_count, SEQ, HEAD
        )
        scores = ATTENTION_SCALE * jnp.einsum(
            "bqgd,bpd->bgqp", query_block, key_block, preferred_element_type=F32
        )
        scores = jnp.where(visible_heads, scores, MASKED)
        highest = jnp.max(scores, axis=-1, keepdims=True)
        raised = jnp.exp(scores - highest)
        totals = jnp.sum(raised, axis=-1, keepdims=True)
        shares = (raised / totals).astype(BF)
        lse_parts.append(highest + jnp.log(totals))
        mixed_parts.append(
            jnp.einsum(
                "bgqp,bpd->bqgd", shares, value_block, preferred_element_type=F32
            ).reshape(length, group_width)
        )
    mixed_heads = jnp.concatenate(mixed_parts, axis=1).astype(BF)
    projected = jnp.dot(mixed_heads, full_output, preferred_element_type=F32)
    residual = inputs + RESIDUAL_SCALE * projected
    scale_two = lax.rsqrt(jnp.mean(residual * residual, axis=-1, keepdims=True) + NORM_EPS)
    normed_two = (residual * scale_two * gain_two).astype(BF)

    normed_blocks = jnp.stack(gather_exp(normed_two))
    logits = jnp.einsum("std,de->ste", normed_blocks, full_router, preferred_element_type=F32)
    expert_ids = jnp.arange(experts, dtype=jnp.int32)
    used = jnp.any(route_blocks[:, :, :, None] == expert_ids, axis=2)
    chosen = jnp.where(used, logits, MASKED)
    raised_gate = jnp.where(used, jnp.exp(chosen - jnp.max(chosen, axis=-1, keepdims=True)), 0.0)
    shares_all = raised_gate / jnp.sum(raised_gate, axis=-1, keepdims=True)
    used_here = lax.dynamic_slice_in_dim(used, me * EXP_DEV, EXP_DEV, 2)
    shares_here = lax.dynamic_slice_in_dim(shares_all, me * EXP_DEV, EXP_DEV, 2)
    block_rows = jnp.arange(length, dtype=jnp.int32)
    before = (block_rows[None, :] < block_rows[:, None]).astype(BF)
    slot = jnp.einsum("tr,sre->ste", before, used_here.astype(BF), preferred_element_type=F32)
    slot = jnp.where(used_here, slot.astype(jnp.int32), -1)
    slot_ids = jnp.arange(CAP, dtype=jnp.int32)
    hit = slot.transpose(2, 0, 1)[:, :, None, :] == slot_ids[None, None, :, None]
    select = hit.astype(BF)
    share_slot = jnp.sum(
        jnp.where(hit, shares_here.transpose(2, 0, 1)[:, :, None, :], 0.0), axis=-1
    )
    rows = owners * CAP
    arrived = (
        jnp.einsum("esct,std->escd", select, normed_blocks, preferred_element_type=F32)
        .astype(BF)
        .reshape(EXP_DEV, rows, D)
    )
    arrived_grads = (
        (
            jnp.einsum("esct,std->escd", select, upstream_blocks, preferred_element_type=F32)
            * (RESIDUAL_SCALE * share_slot[..., None])
        )
        .astype(BF)
        .reshape(EXP_DEV, rows, D)
    )
    gate_value = jnp.einsum("erd,edf->erf", arrived, gate_full, preferred_element_type=F32)
    up_value = jnp.einsum("erd,edf->erf", arrived, up_full, preferred_element_type=F32)
    gate_sigmoid = jax.nn.sigmoid(gate_value)
    activated = gate_value * gate_sigmoid
    hidden = (activated * up_value).astype(BF)
    weighted_out = (
        jnp.einsum("erf,efd->erd", hidden, down_full, preferred_element_type=F32)
        * share_slot.reshape(EXP_DEV, rows, 1)
    ).astype(BF)
    mixture_parts = jnp.einsum(
        "esct,escd->std",
        select,
        weighted_out.reshape(EXP_DEV, owners, CAP, D),
        preferred_element_type=F32,
    )
    mixture = scatter_exp([mixture_parts[j] for j in range(owners)])
    block_out = (residual + RESIDUAL_SCALE * mixture).astype(BF)

    hidden_grad = jnp.einsum(
        "erd,efd->erf", arrived_grads, down_full, preferred_element_type=F32
    )
    down_w_grad = jnp.einsum(
        "erf,erd->efd", hidden, arrived_grads, preferred_element_type=F32
    ).astype(BF)
    pull_slot = jnp.sum(hidden_grad * hidden.astype(F32), axis=-1).reshape(
        EXP_DEV, owners, CAP, 1
    )
    pull_here = jnp.sum(jnp.where(hit, pull_slot, 0.0), axis=2)
    pull = jnp.zeros((experts, length), F32)
    for j in range(owners):
        piece_j = pull_here[:, j]
        if j:
            piece_j = lax.ppermute(
                piece_j, "exp", [(i, i ^ j) for i in range(owners)]
            )
        pull = lax.dynamic_update_slice_in_dim(pull, piece_j, (me ^ j) * EXP_DEV, 0)
    pull = pull.T
    logit_grad = (pull - shares_all[0] * jnp.sum(pull, axis=-1, keepdims=True)).astype(BF)
    gate_pre_grad = (
        hidden_grad * up_value * gate_sigmoid * (1.0 + gate_value * (1.0 - gate_sigmoid))
    ).astype(BF)
    up_pre_grad = (hidden_grad * activated).astype(BF)
    gate_w_grad = jnp.einsum(
        "erd,erf->edf", arrived, gate_pre_grad, preferred_element_type=F32
    ).astype(BF)
    up_w_grad = jnp.einsum(
        "erd,erf->edf", arrived, up_pre_grad, preferred_element_type=F32
    ).astype(BF)
    row_grads = (
        jnp.einsum("erf,edf->erd", gate_pre_grad, gate_full, preferred_element_type=F32)
        + jnp.einsum("erf,edf->erd", up_pre_grad, up_full, preferred_element_type=F32)
    ).astype(BF)
    back_parts = jnp.einsum(
        "esct,escd->std",
        select,
        row_grads.reshape(EXP_DEV, owners, CAP, D),
        preferred_element_type=F32,
    )
    normed_two_grad = scatter_exp([back_parts[j] for j in range(owners)])
    down_sum = lax.psum_scatter(down_w_grad, "fsdp", scatter_dimension=1, tiled=True)
    gate_sum = lax.psum_scatter(gate_w_grad, "fsdp", scatter_dimension=1, tiled=True)
    up_sum = lax.psum_scatter(up_w_grad, "fsdp", scatter_dimension=1, tiled=True)

    upstream = cotangent.astype(F32)
    normed_two_grad = normed_two_grad + jnp.einsum(
        "te,de->td", logit_grad, full_router, preferred_element_type=F32
    )
    router_w_grad = jnp.einsum("td,te->de", normed_two, logit_grad, preferred_element_type=F32)
    inner_two = normed_two_grad * gain_two
    expert_gain_grad = jnp.sum(normed_two_grad * residual * scale_two, axis=0)
    cube_two = scale_two * scale_two * scale_two
    residual_grad = (
        upstream
        + scale_two * inner_two
        - residual * cube_two * jnp.mean(inner_two * residual, axis=-1, keepdims=True)
    )
    proj_grad = (RESIDUAL_SCALE * residual_grad).astype(BF)
    output_w_grad = jnp.einsum("tf,td->fd", mixed_heads, proj_grad, preferred_element_type=F32)
    mixed_grad = jnp.einsum(
        "td,fd->tf", proj_grad, full_output, preferred_element_type=F32
    ).astype(BF)
    query_parts = []
    key_parts = []
    value_parts = []
    for head_group in range(KV_HEADS):
        query_block = queries_rot[
            :, head_group * group_width : (head_group + 1) * group_width
        ].reshape(seq_count, SEQ, group_size, HEAD)
        key_block = keys_rot[:, head_group * HEAD : (head_group + 1) * HEAD].reshape(
            seq_count, SEQ, HEAD
        )
        value_block = values[:, head_group * HEAD : (head_group + 1) * HEAD].reshape(
            seq_count, SEQ, HEAD
        )
        grad_block = mixed_grad[
            :, head_group * group_width : (head_group + 1) * group_width
        ].reshape(seq_count, SEQ, group_size, HEAD)
        scores = ATTENTION_SCALE * jnp.einsum(
            "bqgd,bpd->bgqp", query_block, key_block, preferred_element_type=F32
        )
        scores = jnp.where(visible_heads, scores, MASKED)
        shares_float = jnp.exp(scores - lse_parts[head_group])
        shares = shares_float.astype(BF)
        share_grad = jnp.einsum(
            "bqgd,bpd->bgqp", grad_block, value_block, preferred_element_type=F32
        )
        row_delta = jnp.sum(shares_float * share_grad, axis=-1, keepdims=True)
        score_grad = (shares_float * (share_grad - row_delta)).astype(BF)
        query_parts.append(
            ATTENTION_SCALE
            * jnp.einsum(
                "bgqp,bpd->bqgd", score_grad, key_block, preferred_element_type=F32
            ).reshape(length, group_width)
        )
        key_parts.append(
            ATTENTION_SCALE
            * jnp.einsum(
                "bgqp,bqgd->bpd", score_grad, query_block, preferred_element_type=F32
            ).reshape(length, HEAD)
        )
        value_parts.append(
            jnp.einsum(
                "bgqp,bqgd->bpd", shares, grad_block, preferred_element_type=F32
            ).reshape(length, HEAD)
        )
    query_grad = (
        unrotate(
            jnp.concatenate(query_parts, axis=1).reshape(seq_count, SEQ, HEADS, HEAD),
            cosine,
            sine_table,
        )
        .reshape(length, HEADS * HEAD)
        .astype(BF)
    )
    key_grad = (
        unrotate(
            jnp.concatenate(key_parts, axis=1).reshape(seq_count, SEQ, KV_HEADS, HEAD),
            cosine,
            sine_table,
        )
        .reshape(length, KV_HEADS * HEAD)
        .astype(BF)
    )
    value_grad = jnp.concatenate(value_parts, axis=1).astype(BF)
    qkv_grad = jnp.concatenate([query_grad, key_grad, value_grad], axis=1)
    qkv_w_grad = jnp.einsum("td,tf->df", normed_one, qkv_grad, preferred_element_type=F32)
    normed_one_grad = jnp.einsum("tf,df->td", qkv_grad, full_qkv, preferred_element_type=F32)
    inner_one = normed_one_grad * gain_one
    attention_gain_grad = jnp.sum(normed_one_grad * inputs * scale_one, axis=0)
    cube_one = scale_one * scale_one * scale_one
    input_grad = (
        residual_grad
        + scale_one * inner_one
        - inputs * cube_one * jnp.mean(inner_one * inputs, axis=-1, keepdims=True)
    )

    def piece_sum(grad):
        shaped = grad.reshape(shards, owners * piece, grad.shape[1])
        return scatter_exp(
            [
                lax.dynamic_slice_in_dim(shaped, (me ^ j) * piece, piece, 1)
                for j in range(owners)
            ]
        ).astype(BF)

    misc_grad = jnp.concatenate(
        [
            router_w_grad,
            attention_gain_grad[:, None],
            expert_gain_grad[:, None],
            jnp.zeros((D, MISC - experts - 2), F32),
        ],
        axis=1,
    )
    dense_sums = jnp.concatenate(
        [piece_sum(qkv_w_grad), piece_sum(misc_grad), piece_sum(output_w_grad)], axis=2
    )
    dense_part = lax.psum_scatter(dense_sums, "fsdp", scatter_dimension=0, tiled=True)
    dense_sum = ordered(gather_exp(dense_part[0]), me, 0).astype(F32)
    edges = [HEADS * HEAD, (HEADS + KV_HEADS) * HEAD, QKV, first_cols]
    query_sum, key_sum, value_sum, misc_sum, output_sum = jnp.split(dense_sum, edges, axis=1)
    return (
        block_out,
        input_grad,
        misc_sum[:, experts],
        misc_sum[:, experts + 1],
        query_sum,
        key_sum,
        value_sum,
        output_sum,
        misc_sum[:, :experts],
        gate_sum.astype(F32),
        up_sum.astype(F32),
        down_sum.astype(F32),
    )


def solution(mesh):
    in_specs = (
        P(("exp", "fsdp"), None),
        P(("exp", "fsdp"), None),
        P(("exp", "fsdp")),
        P(("exp", "fsdp"), None),
        P("fsdp"),
        P("fsdp"),
        P("fsdp", None),
        P("fsdp", None),
        P("fsdp", None),
        P("fsdp", None),
        P("fsdp", None),
        P("exp", "fsdp", None),
        P("exp", "fsdp", None),
        P("exp", "fsdp", None),
    )
    out_specs = (
        P(("exp", "fsdp"), None),
        P(("exp", "fsdp"), None),
        P("fsdp"),
        P("fsdp"),
        P("fsdp", None),
        P("fsdp", None),
        P("fsdp", None),
        P("fsdp", None),
        P("fsdp", None),
        P("exp", "fsdp", None),
        P("exp", "fsdp", None),
        P("exp", "fsdp", None),
    )
    return jax.shard_map(
        on_device, mesh=mesh, in_specs=in_specs, out_specs=out_specs, check_vma=False
    )
```

time: 2280 us -> 1220 us (0.54)
  waiting for transfers between devices: 1780 us -> 793 us
  blocking collectives: 114 us -> 0 us
  matrix products: 172 us -> 206 us
    reduce_scatter x4 -> x1, waiting for transfers between devices: 441 us -> 37.7 us  [on_device(): lax.psum_scatter(dense_sums, 'fsdp', scatter_dimension=0, tiled=True)]
    all_gather x7 -> x4, waiting for transfers between devices: 407 us -> 213 us  [the longest x1 106 us: on_device(): down_full = lax.all_gather(down_weight, 'fsdp', axis=1, tiled=True)]
    ppermute x0 -> x31, waiting for transfers between devices: none -> 181 us  [the longest x28 181 us: swap(): return lax.ppermute(values, 'exp', [(i, i ^ bit) for i in range(size)])]
    reduce_scatter x1, waiting for transfers between devices: 255 us -> 78.9 us  [on_device(): lax.psum_scatter(down_w_grad, 'fsdp', scatter_dimension=1, tiled=True)]
    all_to_all x4 -> x0, waiting for transfers between devices: 133 us -> none  [the longest x1 60.1 us: on_device(): lax.all_to_all(row_grads.reshape(owners, EXP_DEV * CAP, D), 'exp', split_...]
    reduce_scatter x1, waiting for transfers between devices: 254 us -> 140 us  [on_device(): lax.psum_scatter(up_w_grad, 'fsdp', scatter_dimension=1, tiled=True)]
    reduce_scatter x1, waiting for transfers between devices: 254 us -> 140 us  [on_device(): lax.psum_scatter(gate_w_grad, 'fsdp', scatter_dimension=1, tiled=True)]
    gather x4 -> x0, local copies, waits for them, and re-layouts: 64.7 us -> none  [the longest x1 20 us: on_device(): outgoing_grads = padded_grads[sources].reshape(owners, EXP_DEV * CAP, D)]
  transfers between devices with their start and end apart: 20 -> 39, of which waited for: 18 -> 19; matrix products, arithmetic and copies ran while one was open for 10% -> 20% of each run, Pallas kernels for 0% -> 0%
where the time goes in v1:
time: 1220 us; the launch traced here: 1200 us
  waiting for transfers between devices  793 us (65%)
  matrix products  206 us (17%)
  local copies, waits for them, and re-layouts  121 us (10%)
  other arithmetic  48.8 us (4%)
  starting transfers between devices  19.3 us (2%)
  between operations  17.2 us (1%)
    ppermute x28, waiting for transfers between devices, swap(): return lax.ppermute(values, 'exp', [(i, i ^ bit) for i in range(size)])  181 us
    reduce_scatter x1, waiting for transfers between devices, on_device(): lax.psum_scatter(gate_w_grad, 'fsdp', scatter_dimension=1, tiled=True)  140 us
    reduce_scatter x1, waiting for transfers between devices, on_device(): lax.psum_scatter(up_w_grad, 'fsdp', scatter_dimension=1, tiled=True)  140 us
    all_gather x1, waiting for transfers between devices, on_device(): down_full = lax.all_gather(down_weight, 'fsdp', axis=1, tiled=True)  106 us
    reduce_scatter x1, waiting for transfers between devices, on_device(): lax.psum_scatter(down_w_grad, 'fsdp', scatter_dimension=1, tiled=True)  78.9 us
    all_gather x1, waiting for transfers between devices, on_device(): dense_quarter = lax.all_gather(dense_piece, 'fsdp', axis=0, tiled=False)  62.4 us
    dynamic_update_slice x10, local copies, waits for them, and re-layouts, ordered(): out = lax.dynamic_update_slice_in_dim(out, block, (me ^ j) * width, axis)  48.4 us
    all_gather x1, waiting for transfers between devices, on_device(): gate_full = lax.all_gather(gate_weight, 'fsdp', axis=1, tiled=True)  44.8 us
  transfers between devices with their start and end apart: 39, of which 19 were waited for; matrix products, arithmetic and copies ran while one was open for 20% of the time, Pallas kernels for 0%

profile of v1, /device:TPU:0, one launch (start us, length us, event | category | flops | bytes accessed | tf_op | source)
XLA Modules:
  0.0 1205.0 jit_solution(1905549702825056736)
XLA Ops:
  15.5 62.4 %all-gather.12.cloned.1.call-done = bf16[384,4224]{1,0:T(8,128)(2,1)} async-done(((bf16[48,4224]{1,0:T(8,128)(2,1)}), bf16[384,4224]{1,0:T(8,128)(2,1)}) %all-gather.12.cloned.1.call-update) | async-done | bytes 3244048 | tf_op jit(solution)/shard_map/all_gather | solution.py:135
  94.3 37.0 %collective-permute-done.7 = s32[256,8]{0,1:T(8,128)S(1)} collective-permute-done((s32[256,8]{0,1:T(8,128)S(1)}, s32[256,8]{0,1:T(8,128)S(1)}, u32[]{:S(2)}, u32[]{:S(2)}) %collective-permute-start.7) | collective-permute-done | bytes 8224 | tf_op jit(solution)/shard_map/ppermute | solution.py:62
  137.5 19.2 %collective-permute-done.4 = bf16[8,48,1536]{2,1,0:T(8,128)(2,1)} collective-permute-done((bf16[8,48,1536]{2,1,0:T(8,128)(2,1)}, bf16[8,48,1536]{2,1,0:T(8,128)(2,1)}, u32[]{:S(2)}, u32[]{:S(2)}) %collective-permute-start.4) | collective-permute-done | bytes 1179680 | tf_op jit(solution)/shard_map/ppermute | solution.py:62
  204.3 17.5 %collective-permute-done.10 = bf16[256,1536]{1,0:T(8,128)(2,1)S(1)} collective-permute-done((bf16[256,1536]{1,0:T(8,128)(2,1)S(1)}, bf16[256,1536]{1,0:T(8,128)(2,1)S(1)}, u32[]{:S(2)}, u32[]{:S(2)}) %collective-permute-start.10) | collective-permute-done | bytes 786464 | tf_op jit(solution)/shard_map/ppermute | solution.py:62
  258.0 12.2 %fusion.220 = f32[5,512,512]{1,2,0:T(8,128)} fusion(bf16[5,512,1536]{2,1,0:T(8,128)(2,1)} %bitcast.681, bf16[5,1536,512]{2,1,0:T(8,128)(2,1)} %all-gather.8.cloned.1.call-done), kind=kOutput, calls=%fused_computation.449 | convolution fusion | flops 4026531840 | bytes 20971520 | tf_op jit(solution)/shard_map/erd,edf->erf/dot_general | solution.py:238
  270.3 44.8 %all-gather.6.cloned.1.call-done = bf16[5,1536,512]{2,1,0:T(8,128)(2,1)} async-done(((bf16[5,192,512]{2,1,0:T(8,128)(2,1)}), bf16[5,1536,512]{2,1,0:T(8,128)(2,1)}) %all-gather.6.cloned.1.call-update) | async-done | bytes 7864336 | tf_op jit(solution)/shard_map/all_gather | solution.py:143
  315.1 12.0 fusion.219
  327.1 106.2 %all-gather.10.cloned.1.call-done = bf16[5,512,1536]{2,1,0:T(8,128)(2,1)} async-done(((bf16[5,64,1536]{2,1,0:T(8,128)(2,1)}), bf16[5,512,1536]{2,1,0:T(8,128)(2,1)}) %all-gather.10.cloned.1.call-update) | async-done | bytes 7864336 | tf_op jit(solution)/shard_map/all_gather | solution.py:145
  433.3 25.0 %multiply_reduce_fusion = (f32[5,512]{1,0:T(8,128)}, bf16[5,512,512]{1,2,0:T(8,128)(2,1)}, bf16[5,512,512]{1,2,0:T(8,128)(2,1)}, bf16[5,512,512]{1,2,0:T(8,128)(2,1)}) fusion(f32[5,512,512]{1,2,0:T(8,128)} %fusion.220, f32[5,512,512]{1,2,0:T(8,128)} %fusion.219, bf16[5,512,1536]{2,1,0:T(8,128)(2,1)} %bitcast.685, ...), kind=kOutput, calls=%fused_computation.17 | convolution fusion | flops 4050122240 | bytes 34088960 | tf_op jit(solution)/shard_map/erd,efd->erf/dot_general | solution.py:255
  472.0 13.9 %fusion.221 = f32[5,512,1536]{2,1,0:T(8,128)} fusion(bf16[5,512,512]{1,2,0:T(8,128)(2,1)} %get-tuple-element.94, bf16[5,1536,512]{2,1,0:T(8,128)(2,1)} %all-gather.6.cloned.1.call-done), kind=kOutput, calls=%fused_computation.450 | convolution fusion | flops 4026531840 | bytes 26214400 | tf_op jit(solution)/shard_map/erf,edf->erd/dot_general | solution.py:286
  485.9 12.9 %add_convert_fusion = bf16[5,512,1536]{2,1,0:T(8,128)(2,1)} fusion(f32[5,512,1536]{2,1,0:T(8,128)} %fusion.221, bf16[5,512,512]{1,2,0:T(8,128)(2,1)} %get-tuple-element.95, bf16[5,1536,512]{2,1,0:T(8,128)(2,1)} %all-gather.8.cloned.1.call-done), kind=kOutput, calls=%fused_computation.3 | convolution fusion | flops 4034396160 | bytes 34078720 | tf_op jit(solution)/shard_map/erf,edf->erd/dot_general | solution.py:287
  522.0 14.8 %collective-permute-done.18 = bf16[256,1536]{1,0:T(8,128)(2,1)} collective-permute-done((bf16[256,1536]{1,0:T(8,128)(2,1)}, bf16[256,1536]{1,0:T(8,128)(2,1)}, u32[]{:S(2)}, u32[]{:S(2)}) %collective-permute-start.18) | collective-permute-done | bytes 786464 | tf_op jit(solution)/shard_map/ppermute | solution.py:62
  539.5 13.6 %collective-permute-done.13 = bf16[256,1536]{1,0:T(8,128)(2,1)S(1)} collective-permute-done((bf16[256,1536]{1,0:T(8,128)(2,1)S(1)}, bf16[256,1536]{1,0:T(8,128)(2,1)S(1)}, u32[]{:S(2)}, u32[]{:S(2)}) %collective-permute-start.13) | collective-permute-done | bytes 786464 | tf_op jit(solution)/shard_map/ppermute | solution.py:62
  620.5 64.1 %collective-permute-done.25 = bf16[8,48,128]{2,1,0:T(8,128)(2,1)S(1)} collective-permute-done((bf16[8,48,128]{2,1,0:T(8,128)(2,1)S(1)}, bf16[8,48,128]{2,1,0:T(8,128)(2,1)S(1)}, u32[]{:S(2)}, u32[]{:S(2)}) %collective-permute-start.25) | collective-permute-done | bytes 98336 | tf_op jit(solution)/shard_map/ppermute | solution.py:62
  692.8 11.4 convolution_convert_fusion
  704.2 11.9 convolution_convert_fusion.2
  716.4 11.9 convolution_convert_fusion.1
  728.3 37.7 %reduce-scatter.5.cloned.1.call-done = bf16[1,48,4224]{2,1,0:T(8,128)(2,1)} async-done(((bf16[8,48,4224]{2,1,0:T(8,128)(2,1)}), bf16[1,48,4224]{2,1,0:T(8,128)(2,1)}) %reduce-scatter.5.cloned.1.call-update) | async-done | bytes 405520 | tf_op jit(solution)/shard_map/reduce_scatter | solution.py:414
  767.4 8.8 collective-permute-done.29
  788.7 9.4 dynamic_update_slice.61
  799.7 9.4 dynamic_update_slice.62
  830.1 78.9 %reduce-scatter.11.cloned.1.call-done = bf16[5,64,1536]{2,1,0:T(8,128)(2,1)} async-done(((bf16[5,512,1536]{2,1,0:T(8,128)(2,1)}), bf16[5,64,1536]{2,1,0:T(8,128)(2,1)}) %reduce-scatter.11.cloned.1.call-update) | async-done | bytes 983056 | tf_op jit(solution)/shard_map/reduce_scatter | solution.py:296
  911.7 140.2 %reduce-scatter.7.cloned.1.call-done = bf16[5,192,512]{2,1,0:T(8,128)(2,1)} async-done(((bf16[5,1536,512]{2,1,0:T(8,128)(2,1)}), bf16[5,192,512]{2,1,0:T(8,128)(2,1)}) %reduce-scatter.7.cloned.1.call-update) | async-done | bytes 983056 | tf_op jit(solution)/shard_map/reduce_scatter | solution.py:297
  1054.7 140.2 %reduce-scatter.9.cloned.1.call-done = bf16[5,192,512]{2,1,0:T(8,128)(2,1)} async-done(((bf16[5,1536,512]{2,1,0:T(8,128)(2,1)}), bf16[5,192,512]{2,1,0:T(8,128)(2,1)}) %reduce-scatter.9.cloned.1.call-update) | async-done | bytes 983056 | tf_op jit(solution)/shard_map/reduce_scatter | solution.py:298
  (435 shorter events, 272.6 us)
Async XLA Ops:
  7.2 70.8 %all-gather.12.cloned.1.call-start = ((), (), s32[]{:S(2)}) async-start(), calls=%async_computation.11 | async-start | bytes 3649536 | tf_op jit(solution)/shard_map/all_gather | solution.py:135
  14.0 244.1 %all-gather.8.cloned.1.call-start = ((), (), s32[]{:S(2)}) async-start(), calls=%async_computation.5 | async-start | bytes 8847360 | tf_op jit(solution)/shard_map/all_gather | solution.py:144
  14.7 300.4 %all-gather.6.cloned.1.call-start = ((), (), s32[]{:S(2)}) async-start(), calls=%async_computation.4 | async-start | bytes 8847360 | tf_op jit(solution)/shard_map/all_gather | solution.py:143
  15.5 417.8 %all-gather.10.cloned.1.call-start = ((), (), s32[]{:S(2)}) async-start(), calls=%async_computation.6 | async-start | bytes 8847360 | tf_op jit(solution)/shard_map/all_gather | solution.py:145
  83.3 48.0 %collective-permute-start.1 = (bf16[8,48,2688]{2,1,0:T(8,128)(2,1)S(1)}, bf16[8,48,2688]{2,1,0:T(8,128)(2,1)}, u32[]{:S(2)}, u32[]{:S(2)}) collective-permute-start(bf16[8,48,2688]{2,1,0:T(8,128)(2,1)S(1)} %get-tuple-element.100), channel_id=1, source_target_pairs={{0,16},{8,24},{16,0},{24,8},{1,17},{9,25},{17,1},{25,9},{2,18},{10... | collective-permute-start | bytes 6193160 | tf_op jit(solution)/shard_map/ppermute | solution.py:62
  84.8 46.4 %collective-permute-start.7 = (s32[256,8]{0,1:T(8,128)S(1)}, s32[256,8]{0,1:T(8,128)S(1)}, u32[]{:S(2)}, u32[]{:S(2)}) collective-permute-start(s32[256,8]{0,1:T(8,128)S(1)} %copy-done.65), channel_id=1, source_target_pairs={{0,16},{8,24},{16,0},{24,8},{1,17},{9,25},{17,1},{25,9},{2,18},{10... | collective-permute-start | bytes 24584 | tf_op jit(solution)/shard_map/ppermute | solution.py:62
  85.3 680.6 %reduce-scatter.5.cloned.1.call-start = ((), (), s32[]{:S(2)}) async-start(), calls=%async_computation.7 | async-start | bytes 3649536 | tf_op jit(solution)/shard_map/reduce_scatter | solution.py:414
  85.4 76.1 %collective-permute-start = (bf16[8,48,2688]{2,1,0:T(8,128)(2,1)S(1)}, bf16[8,48,2688]{2,1,0:T(8,128)(2,1)}, u32[]{:S(2)}, u32[]{:S(2)}) collective-permute-start(bf16[8,48,2688]{2,1,0:T(8,128)(2,1)S(1)} %get-tuple-element.100), channel_id=1, source_target_pairs={{0,8},{8,0},{16,24},{24,16},{1,9},{9,1},{17,25},{25,17},{2,10},{10... | collective-permute-start | bytes 6193160 | tf_op jit(solution)/shard_map/ppermute | solution.py:62
  91.2 46.2 %collective-permute-start.3 = (bf16[8,48,1536]{2,1,0:T(8,128)(2,1)}, bf16[8,48,1536]{2,1,0:T(8,128)(2,1)}, u32[]{:S(2)}, u32[]{:S(2)}) collective-permute-start(bf16[8,48,1536]{2,1,0:T(8,128)(2,1)} %get-tuple-element.98), channel_id=1, source_target_pairs={{0,8},{8,0},{16,24},{24,16},{1,9},{9,1},{17,25},{25,17},{2,10},{10... | collective-permute-start | bytes 3538952 | tf_op jit(solution)/shard_map/ppermute | solution.py:62
  91.7 64.9 %collective-permute-start.4 = (bf16[8,48,1536]{2,1,0:T(8,128)(2,1)}, bf16[8,48,1536]{2,1,0:T(8,128)(2,1)}, u32[]{:S(2)}, u32[]{:S(2)}) collective-permute-start(bf16[8,48,1536]{2,1,0:T(8,128)(2,1)} %get-tuple-element.98), channel_id=1, source_target_pairs={{0,16},{8,24},{16,0},{24,8},{1,17},{9,25},{17,1},{25,9},{2,18},{10... | collective-permute-start | bytes 3538952 | tf_op jit(solution)/shard_map/ppermute | solution.py:62
  131.3 37.5 %collective-permute-start.2 = (bf16[8,48,2688]{2,1,0:T(8,128)(2,1)}, bf16[8,48,2688]{2,1,0:T(8,128)(2,1)}, u32[]{:S(2)}, u32[]{:S(2)}) collective-permute-start(bf16[8,48,2688]{2,1,0:T(8,128)(2,1)} %collective-permute-done.1), channel_id=1, source_target_pairs={{0,8},{8,0},{16,24},{24,16},{1,9},{9,1},{17,25},{25,17},{2,10},{10... | collective-permute-start | bytes 6193160 | tf_op jit(solution)/shard_map/ppermute | solution.py:62
  135.9 67.8 %collective-permute-start.15 = (bf16[256,1536]{1,0:T(8,128)(2,1)}, bf16[256,1536]{1,0:T(8,128)(2,1)}, u32[]{:S(2)}, u32[]{:S(2)}) collective-permute-start(bf16[256,1536]{1,0:T(8,128)(2,1)} %param.15), channel_id=1, source_target_pairs={{0,16},{8,24},{16,0},{24,8},{1,17},{9,25},{17,1},{25,9},{2,18},{10... | collective-permute-start | bytes 2359304 | tf_op jit(solution)/shard_map/ppermute | solution.py:62
  137.4 106.1 %collective-permute-start.14 = (bf16[256,1536]{1,0:T(8,128)(2,1)}, bf16[256,1536]{1,0:T(8,128)(2,1)}, u32[]{:S(2)}, u32[]{:S(2)}) collective-permute-start(bf16[256,1536]{1,0:T(8,128)(2,1)} %param.15), channel_id=1, source_target_pairs={{0,8},{8,0},{16,24},{24,16},{1,9},{9,1},{17,25},{25,17},{2,10},{10... | collective-permute-start | bytes 2359304 | tf_op jit(solution)/shard_map/ppermute | solution.py:62
  201.9 19.9 %collective-permute-start.10 = (bf16[256,1536]{1,0:T(8,128)(2,1)S(1)}, bf16[256,1536]{1,0:T(8,128)(2,1)S(1)}, u32[]{:S(2)}, u32[]{:S(2)}) collective-permute-start(bf16[256,1536]{1,0:T(8,128)(2,1)S(1)} %multiply_convert_fusion.5), channel_id=1, source_target_pairs={{0,16},{8,24},{16,0},{24,8},{1,17},{9,25},{17,1},{25,9},{2,18},{10... | collective-permute-start | bytes 2359304 | tf_op jit(solution)/shard_map/ppermute | solution.py:62
  203.7 39.8 %collective-permute-start.16 = (bf16[256,1536]{1,0:T(8,128)(2,1)}, bf16[256,1536]{1,0:T(8,128)(2,1)}, u32[]{:S(2)}, u32[]{:S(2)}) collective-permute-start(bf16[256,1536]{1,0:T(8,128)(2,1)} %collective-permute-done.15), channel_id=1, source_target_pairs={{0,8},{8,0},{16,24},{24,16},{1,9},{9,1},{17,25},{25,17},{2,10},{10... | collective-permute-start | bytes 2359304 | tf_op jit(solution)/shard_map/ppermute | solution.py:62
  516.1 20.7 %collective-permute-start.18 = (bf16[256,1536]{1,0:T(8,128)(2,1)}, bf16[256,1536]{1,0:T(8,128)(2,1)}, u32[]{:S(2)}, u32[]{:S(2)}) collective-permute-start(bf16[256,1536]{1,0:T(8,128)(2,1)} %fusion.110), channel_id=1, source_target_pairs={{0,16},{8,24},{16,0},{24,8},{1,17},{9,25},{17,1},{25,9},{2,18},{10... | collective-permute-start | bytes 2359304 | tf_op jit(solution)/shard_map/ppermute | solution.py:62
  520.6 32.5 %collective-permute-start.13 = (bf16[256,1536]{1,0:T(8,128)(2,1)S(1)}, bf16[256,1536]{1,0:T(8,128)(2,1)S(1)}, u32[]{:S(2)}, u32[]{:S(2)}) collective-permute-start(bf16[256,1536]{1,0:T(8,128)(2,1)S(1)} %fusion.109), channel_id=1, source_target_pairs={{0,16},{8,24},{16,0},{24,8},{1,17},{9,25},{17,1},{25,9},{2,18},{10... | collective-permute-start | bytes 2359304 | tf_op jit(solution)/shard_map/ppermute | solution.py:62
  612.3 74.8 %collective-permute-start.23 = (bf16[8,48,2560]{2,1,0:T(8,128)(2,1)S(1)}, bf16[8,48,2560]{2,1,0:T(8,128)(2,1)S(1)}, u32[]{:S(2)}, u32[]{:S(2)}) collective-permute-start(bf16[8,48,2560]{2,1,0:T(8,128)(2,1)S(1)} %fusion.17), channel_id=1, source_target_pairs={{0,16},{8,24},{16,0},{24,8},{1,17},{9,25},{17,1},{25,9},{2,18},{10... | collective-permute-start | bytes 5898248 | tf_op jit(solution)/shard_map/ppermute | solution.py:62
  616.2 68.4 %collective-permute-start.27 = (bf16[8,48,1536]{2,1,0:T(8,128)(2,1)S(1)}, bf16[8,48,1536]{2,1,0:T(8,128)(2,1)S(1)}, u32[]{:S(2)}, u32[]{:S(2)}) collective-permute-start(bf16[8,48,1536]{2,1,0:T(8,128)(2,1)S(1)} %fusion.27), channel_id=1, source_target_pairs={{0,16},{8,24},{16,0},{24,8},{1,17},{9,25},{17,1},{25,9},{2,18},{10... | collective-permute-start | bytes 3538952 | tf_op jit(solution)/shard_map/ppermute | solution.py:62
  618.9 65.6 %collective-permute-start.25 = (bf16[8,48,128]{2,1,0:T(8,128)(2,1)S(1)}, bf16[8,48,128]{2,1,0:T(8,128)(2,1)S(1)}, u32[]{:S(2)}, u32[]{:S(2)}) collective-permute-start(bf16[8,48,128]{2,1,0:T(8,128)(2,1)S(1)} %fusion.178), channel_id=1, source_target_pairs={{0,16},{8,24},{16,0},{24,8},{1,17},{9,25},{17,1},{25,9},{2,18},{10... | collective-permute-start | bytes 294920 | tf_op jit(solution)/shard_map/ppermute | solution.py:62
  692.5 216.5 %reduce-scatter.11.cloned.1.call-start = ((), (), s32[]{:S(2)}) async-start(), calls=%async_computation.10 | async-start | bytes 8847360 | tf_op jit(solution)/shard_map/reduce_scatter | solution.py:296
  704.1 347.8 %reduce-scatter.7.cloned.1.call-start = ((), (), s32[]{:S(2)}) async-start(), calls=%async_computation.8 | async-start | bytes 8847360 | tf_op jit(solution)/shard_map/reduce_scatter | solution.py:297
  716.1 478.8 %reduce-scatter.9.cloned.1.call-start = ((), (), s32[]{:S(2)}) async-start(), calls=%async_computation.9 | async-start | bytes 8847360 | tf_op jit(solution)/shard_map/reduce_scatter | solution.py:298
  776.2 33.0 %collective-permute-start.30 = (bf16[48,4224]{1,0:T(8,128)(2,1)}, bf16[48,4224]{1,0:T(8,128)(2,1)}, u32[]{:S(2)}, u32[]{:S(2)}) collective-permute-start(bf16[48,4224]{1,0:T(8,128)(2,1)} %collective-permute-done.29), channel_id=1, source_target_pairs={{0,8},{8,0},{16,24},{24,16},{1,9},{9,1},{17,25},{25,17},{2,10},{10... | collective-permute-start | bytes 1216520 | tf_op jit(solution)/shard_map/ppermute | solution.py:62
  (86 other events, 734.6 us)
Sparse Core Ops, SparseCore 0:
  14.1 63.7 all-gather.11
  80.1 116.5 all-gather.7
  199.0 116.0 all-gather.5
  317.1 116.0 all-gather.9
  692.6 73.2 reduce-scatter.4
  769.4 139.5 reduce-scatter.10
  912.6 139.2 reduce-scatter.6
  1055.6 139.2 reduce-scatter.8
